TPU v7x, 128 devices: a whole 4x4x4 slice. The times are simulated.
128 devices in a mesh: row: 16 (over z, y), col: 8 (over x, core).
Axes of the slice: x: 4, y: 4, z: 4, core: 2. Of those that a mesh axis runs over, the one named last changes fastest.
Arguments:
- counts: int32 [2048, 262144], P('row', 'col'), may hold values from 0 to 7, as said below
- row_total: float32 [2048], P('row'), may hold values from 1 to 3670016, as said below
- col_total: float32 [262144], P('col'), may hold values from 1 to 3670272, as said below
- grand_total: float32 [1], replicated, as said below
- sketch: float32 [262144, 96], P(('col', 'row')), may hold values from -0.00024414062 to 0.00024414062
Outputs:
- column_factors: float32 [262144, 96], P(('col', 'row'))
- gram_factor: float32 [96, 96], replicated
Inputs may be any that keep to these rules, and one draw needn't show every extreme that they name: About half of the counts are zero. `row_total`: each row's total is its counts' sum times a factor between 1 and 2. `col_total`: each item's total is its counts' sum over the slab plus one, times 262144 / 2048, times a factor between 1 and 2. `grand_total`: the grand total is the sum of col_total times a factor between 1 and 1.25.
All inputs are finite; a program needn't handle non-finite values.
Results may differ from a plain program's by a relative error of at most 0.0003.
Values sent between devices are 32-bit elements; how exact they have to be, the bound alone decides.
No kernel may reach another device: no remote copies, remote signals or barrier semaphores. Data moves between devices by JAX's collectives and lax.ppermute only.
A program may use at most 128 MiB of HBM per device.

v0:
```python
import jax
import jax.numpy as jnp
from jax import lax
from jax.sharding import Mesh
from jax.sharding import PartitionSpec as P

ROW = ("row_0", "row_1")
COL_ROW = ("col", "row_0", "row_1")


def from_everyone(array, axis):
    copies = jnp.broadcast_to(array, (lax.axis_size(axis), *array.shape))
    return lax.all_to_all(copies, axis, split_axis=0, concat_axis=0, tiled=True)


def over_copies(array, axis):
    return from_everyone(array, axis).sum(axis=0)


def over_axes(array, axes):
    for axis in axes:
        array = lax.psum(array, axis)
    return array


def per_device(counts, row_total, col_total, grand_total, sketch):
    row_log = jnp.log(grand_total[0]) - jnp.log(row_total)
    counts_float = counts.astype(jnp.float32)
    pmi = jnp.log(jnp.maximum(counts_float, 1.0)) + row_log[:, None] - jnp.log(col_total)[None, :]
    ppmi_tile = jnp.where(counts > 0, jnp.maximum(pmi, 0.0), 0.0)
    columns = ppmi_tile
    partial_image = jnp.dot(
        columns,
        lax.all_gather(sketch, ROW, axis=0, tiled=True),
        precision=lax.Precision.HIGHEST,
        preferred_element_type=jnp.float32,
    )
    image = over_copies(partial_image, "col")
    gram_local = jnp.dot(
        image.T, image, precision=lax.Precision.HIGHEST, preferred_element_type=jnp.float32
    )
    gram_matrix = over_axes(gram_local, ROW)
    factor = jnp.linalg.cholesky(gram_matrix)
    columns = ppmi_tile
    summed_columns = lax.psum_scatter(
        lax.dot_general(
            columns,
            image,
            (((0,), (0,)), ((), ())),
            precision=lax.Precision.HIGHEST,
            preferred_element_type=jnp.float32,
        ),
        ROW,
        scatter_dimension=0,
        tiled=True,
    )
    column_factors = jax.scipy.linalg.solve_triangular(factor, summed_columns.T, lower=True).T
    return (column_factors, factor)


def solution(mesh):
    finer = Mesh(mesh.devices.reshape(4, 4, mesh.shape["col"]), ("row_0", "row_1", "col"))
    placed = (P(ROW, "col"), P(ROW), P("col"), P(), P(COL_ROW, None))
    return jax.shard_map(
        per_device, mesh=finer, in_specs=placed, out_specs=(P(COL_ROW, None), P()), check_vma=False
    )
```

profile of v0, /device:TPU:1, one launch (start us, length us, event | category | flops | bytes accessed | tf_op | source)
XLA Modules:
  0.0 267.4 jit_solution(10332997755704691555)
XLA Ops:
  7.2 0.0 all-gather.2.cloned.1.call-start
  7.2 0.7 all-gather.2.cloned.1.call-update
  7.9 0.0 reduce-scatter.2.cloned.1.call-start
  7.9 0.9 log.19
  9.6 0.7 log_subtract_fusion
  10.2 92.9 %all-gather.2.cloned.1.call-done = f32[32768,96]{0,1:T(8,128)} async-done(((f32[2048,96]{0,1:T(8,128)}), f32[32768,96]{0,1:T(8,128)}) %all-gather.2.cloned.1.call-update) | async-done | bytes 12582928 | tf_op jit(solution)/shard_map/all_gather | solution.py:34
  103.1 25.3 %fusion.1 = f32[128,96]{0,1:T(8,128)S(1)} fusion(f32[32768,96]{0,1:T(8,128)} %all-gather.2.cloned.1.call-done, s32[128,32768]{1,0:T(8,128)} %param.5, f32[32768]{0:T(1024)S(1)} %log.19, f32[128]{0:T(128)S(1)} %log_subtract_fusion), kind=kOutput, calls=%fused_computation.2 | convolution fusion | flops 4861198336 | bytes 29540864 | tf_op jit(solution)/shard_map/dot_general | solution.py:32
  128.5 12.9 %all_to_all.5 = f32[8,128,96]{1,2,0:T(8,128)S(1)} all-to-all(f32[8,128,96]{1,2,0:T(8,128)S(1)} %broadcast_in_dim.5), channel_id=1, replica_groups=mesh['row_0'=4,'row_1'=4,'col'=8] {'col'}, dimensions={0} | all-to-all | bytes 786432 | tf_op jit(solution)/shard_map/all_to_all | solution.py:13
  141.4 23.0 %fusion = f32[32768,96]{0,1:T(8,128)} fusion(f32[128,96]{0,1:T(8,128)S(1)} %reduce_sum.9, s32[128,32768]{1,0:T(8,128)} %param.5, f32[32768]{0:T(1024)S(1)} %log.19, f32[128]{0:T(128)S(1)} %log_subtract_fusion), kind=kOutput, calls=%fused_computation.1 | convolution fusion | flops 4861198336 | bytes 29540864 | tf_op jit(solution)/shard_map/dot_general | solution.py:46
  164.4 0.0 reduce-scatter.2.cloned.1.call-update
  164.4 0.2 fusion.21
  164.7 15.1 %psum.14 = f32[96,96]{0,1:T(8,128)S(1)} all-reduce(f32[96,96]{0,1:T(8,128)S(1)} %fusion.21), channel_id=1, replica_groups=mesh['row_0'=4,'row_1'=4,'col'=8] {'row_0'}, use_global_device_ids=true, to_apply=%region_2.3 | all-reduce | flops 9216 | bytes 73728 | tf_op jit(solution)/shard_map/psum | solution.py:22
  179.7 13.8 %psum.15 = f32[96,96]{0,1:T(8,128)S(1)} all-reduce(f32[96,96]{0,1:T(8,128)S(1)} %psum.14), channel_id=1, replica_groups=mesh['row_0'=4,'row_1'=4,'col'=8] {'row_1'}, use_global_device_ids=true, to_apply=%region_3.4 | all-reduce | flops 9216 | bytes 73728 | tf_op jit(solution)/shard_map/psum | solution.py:22
  193.6 0.1 copy.13
  193.7 8.8 %cholesky.16 = f32[96,96]{1,0:T(8,128)S(1)} custom-call(f32[96,96]{1,0:T(8,128)S(1)} %fusion.14), custom_call_target="Cholesky" | custom-call | tf_op jit(solution)/shard_map/jit(cholesky)/cholesky | solution.py:43
  202.5 0.6 compare_reduce_fusion
  203.1 1.3 select_bitcast_fusion
  204.4 7.4 %custom-call.7 = f32[1,96,96]{1,2,0:T(8,128)S(1)} custom-call(f32[1,96,96]{2,1,0:T(8,128)S(1)} %get-tuple-element.2), custom_call_target="InvertDiagBlocksLowerTriangular" | custom-call | tf_op jit(solution)/shard_map/jit(_solve_triangular)/triangular_solve | solution.py:57
  211.8 46.0 %reduce-scatter.2.cloned.1.call-done = f32[2048,96]{0,1:T(8,128)} async-done(((f32[32768,96]{0,1:T(8,128)}), f32[2048,96]{0,1:T(8,128)}) %reduce-scatter.2.cloned.1.call-update) | async-done | bytes 786448 | tf_op jit(solution)/shard_map/reduce_scatter | solution.py:45
  257.8 2.8 %fusion.12 = f32[2048,96]{0,1:T(8,128)} fusion(f32[2048,96]{0,1:T(8,128)} %reduce-scatter.2.cloned.1.call-done, f32[1,96,96]{1,2,0:T(8,128)S(1)} %custom-call.7), kind=kOutput, calls=%fused_computation.13 | convolution fusion | flops 226492416 | bytes 1609728 | tf_op jit(solution)/shard_map/jit(_solve_triangular)/triangular_solve | solution.py:57
  (4 shorter events, 0.1 us)
Async XLA Ops:
  7.2 95.9 %all-gather.2.cloned.1.call-start = ((), (), s32[]{:S(2)}) async-start(), calls=%async_computation.2 | async-start | bytes 13369344 | tf_op jit(solution)/shard_map/all_gather | solution.py:34
  7.9 249.9 %reduce-scatter.2.cloned.1.call-start = ((), (), s32[]{:S(2)}) async-start(), calls=%async_computation.3 | async-start | bytes 13369344 | tf_op jit(solution)/shard_map/reduce_scatter | solution.py:45
Sparse Core Ops, SparseCore 0:
  10.1 92.9 all-gather.1
  164.5 93.1 reduce-scatter.1
where the time goes:
time: 268 us; the launch traced here: 267 us
  waiting for transfers between devices  140 us (52%)
  matrix products  51.3 us (19%)
  blocking collectives  41.8 us (16%)
  other arithmetic  18.8 us (7%)
  between operations  14.8 us (6%)
    all_gather x1, waiting for transfers between devices, per_device(): lax.all_gather(sketch, ROW, axis=0, tiled=True)  92.9 us
    reduce_scatter x1, waiting for transfers between devices, per_device(): lax.psum_scatter(lax.dot_general(columns, image, (((0,), (0,)), ((), ()))...  46 us
    psum x2, blocking collectives, over_axes(): array = lax.psum(array, axis)  28.9 us
    dot_general x1, matrix products, per_device(): jnp.dot(columns, lax.all_gather(sketch, ROW, axis=0, tiled=True), precisi...  25.3 us
    dot_general x1, matrix products, per_device(): lax.dot_general(columns, image, (((0,), (0,)), ((), ())), precision=lax.P...  23 us
    all_to_all x1, blocking collectives, from_everyone(): return lax.all_to_all(copies, axis, split_axis=0, concat_axis=0, tiled=True)  12.9 us
    another operation x3, other arithmetic, per_device(): factor = jnp.linalg.cholesky(gram_matrix)  9.45 us
    another operation x2, other arithmetic, per_device(): jax.scipy.linalg.solve_triangular(factor, summed_columns.T, lower=True)  8.63 us
  transfers between devices with their start and end apart: 2, of which 2 were waited for; matrix products, arithmetic and copies ran while one was open for 7% of the time, Pallas kernels for 0%

commit v1 on v0

--- a/solution.py
+++ b/solution.py
@@ -19,7 +19,7 @@
 
 def over_axes(array, axes):
     for axis in axes:
-        array = lax.psum(array, axis)
+        array = jnp.sum(lax.all_gather(array, axis), axis=0)
     return array
 
 

time: 268 us -> 268 us (level)
  waiting for transfers between devices: 140 us -> 148 us
  blocking collectives: 41.8 us -> 34.1 us
    psum x2 -> x0, blocking collectives: 28.9 us -> none  [over_axes(): array = lax.psum(array, axis)]
    all_gather x0 -> x2, blocking collectives: none -> 21.2 us  [over_axes(): array = jnp.sum(lax.all_gather(array, axis), axis=0)]
    reduce_scatter x1, waiting for transfers between devices: 46 us -> 54.2 us  [per_device(): lax.psum_scatter(lax.dot_general(columns, image, (((0,), (0,)), ((), ()))...]
where the time goes in v1:
time: 268 us
  waiting for transfers between devices  148 us (55%)
  matrix products  51.3 us (19%)
  blocking collectives  34.1 us (13%)
  other arithmetic  18.8 us (7%)
  between operations  14.8 us (6%)
    all_gather x1, waiting for transfers between devices, per_device(): lax.all_gather(sketch, ROW, axis=0, tiled=True)  92.9 us
    reduce_scatter x1, waiting for transfers between devices, per_device(): lax.psum_scatter(lax.dot_general(columns, image, (((0,), (0,)), ((), ()))...  54.2 us
    dot_general x1, matrix products, per_device(): jnp.dot(columns, lax.all_gather(sketch, ROW, axis=0, tiled=True), precisi...  25.3 us
    dot_general x1, matrix products, per_device(): lax.dot_general(columns, image, (((0,), (0,)), ((), ())), precision=lax.P...  23 us
    all_gather x2, blocking collectives, over_axes(): array = jnp.sum(lax.all_gather(array, axis), axis=0)  21.2 us
    all_to_all x1, blocking collectives, from_everyone(): return lax.all_to_all(copies, axis, split_axis=0, concat_axis=0, tiled=True)  12.9 us
    another operation x3, other arithmetic, per_device(): factor = jnp.linalg.cholesky(gram_matrix)  9.45 us
    another operation x2, other arithmetic, per_device(): jax.scipy.linalg.solve_triangular(factor, summed_columns.T, lower=True)  8.63 us
  transfers between devices with their start and end apart: 2, of which 2 were waited for; matrix products, arithmetic and copies ran while one was open for 7% of the time, Pallas kernels for 0%

profile of v1, /device:TPU:1, one launch (start us, length us, event | category | flops | bytes accessed | tf_op | source)
XLA Modules:
  0.0 267.9 jit_solution(2486787197261087222)
XLA Ops:
  7.2 0.0 all-gather.4.cloned.1.call-start
  7.2 0.7 all-gather.4.cloned.1.call-update
  7.9 0.0 reduce-scatter.2.cloned.1.call-start
  7.9 0.9 log.19
  9.6 0.7 log_subtract_fusion
  10.2 92.9 %all-gather.4.cloned.1.call-done = f32[32768,96]{0,1:T(8,128)} async-done(((f32[2048,96]{0,1:T(8,128)}), f32[32768,96]{0,1:T(8,128)}) %all-gather.4.cloned.1.call-update) | async-done | bytes 12582928 | tf_op jit(solution)/shard_map/all_gather | solution.py:34
  103.1 25.3 %fusion.1 = f32[128,96]{0,1:T(8,128)S(1)} fusion(f32[32768,96]{0,1:T(8,128)} %all-gather.4.cloned.1.call-done, s32[128,32768]{1,0:T(8,128)} %param.5, f32[32768]{0:T(1024)S(1)} %log.19, f32[128]{0:T(128)S(1)} %log_subtract_fusion), kind=kOutput, calls=%fused_computation.2 | convolution fusion | flops 4861198336 | bytes 29540864 | tf_op jit(solution)/shard_map/dot_general | solution.py:32
  128.5 12.9 %all_to_all.5 = f32[8,128,96]{1,2,0:T(8,128)S(1)} all-to-all(f32[8,128,96]{1,2,0:T(8,128)S(1)} %broadcast_in_dim.5), channel_id=1, replica_groups=mesh['row_0'=4,'row_1'=4,'col'=8] {'col'}, dimensions={0} | all-to-all | bytes 786432 | tf_op jit(solution)/shard_map/all_to_all | solution.py:13
  141.4 23.0 %fusion = f32[32768,96]{0,1:T(8,128)} fusion(f32[128,96]{0,1:T(8,128)S(1)} %reduce_sum.27, s32[128,32768]{1,0:T(8,128)} %param.5, f32[32768]{0:T(1024)S(1)} %log.19, f32[128]{0:T(128)S(1)} %log_subtract_fusion), kind=kOutput, calls=%fused_computation.1 | convolution fusion | flops 4861198336 | bytes 29540864 | tf_op jit(solution)/shard_map/dot_general | solution.py:46
  164.4 0.0 reduce-scatter.2.cloned.1.call-update
  164.4 0.2 fusion.21
  164.7 9.8 %all-gather = f32[384,96]{1,0:T(8,128)S(1)} all-gather(f32[96,96]{1,0:T(8,128)S(1)} %fusion.21), channel_id=2, replica_groups=mesh['row_0'=4,'row_1'=4,'col'=8] {'row_0'}, dimensions={0}, use_global_device_ids=true | all-gather | bytes 184320 | tf_op jit(solution)/shard_map/all_gather | solution.py:22
  174.5 11.3 %all-gather.1 = f32[384,96]{1,0:T(8,128)S(1)} all-gather(f32[96,96]{1,0:T(8,128)S(1)} %reduce_sum.28), channel_id=3, replica_groups=mesh['row_0'=4,'row_1'=4,'col'=8] {'row_1'}, dimensions={0}, use_global_device_ids=true | all-gather | bytes 184320 | tf_op jit(solution)/shard_map/all_gather | solution.py:22
  185.9 0.1 copy.11
  186.0 8.8 %cholesky.16 = f32[96,96]{1,0:T(8,128)S(1)} custom-call(f32[96,96]{1,0:T(8,128)S(1)} %fusion.14), custom_call_target="Cholesky" | custom-call | tf_op jit(solution)/shard_map/jit(cholesky)/cholesky | solution.py:43
  194.8 0.6 compare_reduce_fusion
  195.4 1.3 select_bitcast_fusion
  196.7 7.4 %custom-call.7 = f32[1,96,96]{1,2,0:T(8,128)S(1)} custom-call(f32[1,96,96]{2,1,0:T(8,128)S(1)} %get-tuple-element.2), custom_call_target="InvertDiagBlocksLowerTriangular" | custom-call | tf_op jit(solution)/shard_map/jit(_solve_triangular)/triangular_solve | solution.py:57
  204.1 54.2 %reduce-scatter.2.cloned.1.call-done = f32[2048,96]{0,1:T(8,128)} async-done(((f32[32768,96]{0,1:T(8,128)}), f32[2048,96]{0,1:T(8,128)}) %reduce-scatter.2.cloned.1.call-update) | async-done | bytes 786448 | tf_op jit(solution)/shard_map/reduce_scatter | solution.py:45
  258.2 2.8 %fusion.12 = f32[2048,96]{0,1:T(8,128)} fusion(f32[2048,96]{0,1:T(8,128)} %reduce-scatter.2.cloned.1.call-done, f32[1,96,96]{1,2,0:T(8,128)S(1)} %custom-call.7), kind=kOutput, calls=%fused_computation.13 | convolution fusion | flops 226492416 | bytes 1609728 | tf_op jit(solution)/shard_map/jit(_solve_triangular)/triangular_solve | solution.py:57
  (6 shorter events, 0.1 us)
Async XLA Ops:
  7.2 95.9 %all-gather.4.cloned.1.call-start = ((), (), s32[]{:S(2)}) async-start(), calls=%async_computation.2 | async-start | bytes 13369344 | tf_op jit(solution)/shard_map/all_gather | solution.py:34
  7.9 250.3 %reduce-scatter.2.cloned.1.call-start = ((), (), s32[]{:S(2)}) async-start(), calls=%async_computation.3 | async-start | bytes 13369344 | tf_op jit(solution)/shard_map/reduce_scatter | solution.py:45
Sparse Core Ops, SparseCore 0:
  10.1 92.9 all-gather.3
  164.5 93.6 reduce-scatter.1

commit v2 on v0

--- a/solution.py
+++ b/solution.py
@@ -31,7 +31,9 @@
     columns = ppmi_tile
     partial_image = jnp.dot(
         columns,
-        lax.all_gather(sketch, ROW, axis=0, tiled=True),
+        jnp.concatenate(
+            lax.all_to_all(jnp.stack([sketch] * lax.axis_size(ROW)), ROW, 0, 0), axis=0
+        ),
         precision=lax.Precision.HIGHEST,
         preferred_element_type=jnp.float32,
     )

time: 268 us -> 386 us (1.44)
  waiting for transfers between devices: 140 us -> 233 us
  local copies, waits for them, and re-layouts: 1.04 us -> 18.6 us
  starting transfers between devices: 0.08 us -> 8.67 us
    all_to_all x0 -> x1, waiting for transfers between devices: none -> 185 us  [per_device(): lax.all_to_all(jnp.stack([sketch] * lax.axis_size(ROW)), ROW, 0, 0)]
    all_gather x1 -> x0, waiting for transfers between devices: 92.9 us -> none  [per_device(): lax.all_gather(sketch, ROW, axis=0, tiled=True)]
    reshape x0 -> x1, local copies, waits for them, and re-layouts: none -> 11.2 us  [per_device(): jnp.concatenate(lax.all_to_all(jnp.stack([sketch] * lax.axis_size(ROW)),...]
    all_to_all x0 -> x1, starting transfers between devices: none -> 8.63 us  [per_device(): lax.all_to_all(jnp.stack([sketch] * lax.axis_size(ROW)), ROW, 0, 0)]
    another operation x0 -> x1, local copies, waits for them, and re-layouts: none -> 7.23 us  [per_device(): jnp.stack([sketch] * lax.axis_size(ROW))]
  transfers between devices with their start and end apart: 2 -> 2, of which waited for: 2 -> 2; matrix products, arithmetic and copies ran while one was open for 7% -> 5% of each run, Pallas kernels for 0% -> 0%
where the time goes in v2:
time: 386 us; the launch traced here: 385 us
  waiting for transfers between devices  233 us (60%)
  matrix products  51.3 us (13%)
  blocking collectives  40.8 us (11%)
  local copies, waits for them, and re-layouts  18.6 us (5%)
  other arithmetic  18.1 us (5%)
  between operations  14.8 us (4%)
  starting transfers between devices  8.67 us (2%)
    all_to_all x1, waiting for transfers between devices, per_device(): lax.all_to_all(jnp.stack([sketch] * lax.axis_size(ROW)), ROW, 0, 0)  185 us
    reduce_scatter x1, waiting for transfers between devices, per_device(): lax.psum_scatter(lax.dot_general(columns, image, (((0,), (0,)), ((), ()))...  47.4 us
    psum x2, blocking collectives, over_axes(): array = lax.psum(array, axis)  26.9 us
    dot_general x1, matrix products, per_device(): jnp.dot(columns, jnp.concatenate(lax.all_to_all(jnp.stack([sketch] * lax....  25.3 us
    dot_general x1, matrix products, per_device(): lax.dot_general(columns, image, (((0,), (0,)), ((), ())), precision=lax.P...  23 us
    all_to_all x1, blocking collectives, from_everyone(): return lax.all_to_all(copies, axis, split_axis=0, concat_axis=0, tiled=True)  13.9 us
    reshape x1, local copies, waits for them, and re-layouts, per_device(): jnp.concatenate(lax.all_to_all(jnp.stack([sketch] * lax.axis_size(ROW)),...  11.2 us
    another operation x3, other arithmetic, per_device(): factor = jnp.linalg.cholesky(gram_matrix)  9.45 us
  transfers between devices with their start and end apart: 2, of which 2 were waited for; matrix products, arithmetic and copies ran while one was open for 5% of the time, Pallas kernels for 0%

profile of v2, /device:TPU:1, one launch (start us, length us, event | category | flops | bytes accessed | tf_op | source)
XLA Modules:
  0.0 385.3 jit_solution(11962269980898573478)
XLA Ops:
  7.2 0.0 copy-start
  7.2 0.0 copy-start.1
  7.2 7.2 %stack.2 = f32[16,2048,96]{1,2,0:T(8,128)} broadcast(f32[2048,96]{0,1:T(8,128)} %param.9), dimensions={1,2} | broadcast | bytes 13369344 | tf_op jit(solution)/shard_map/stack | solution.py:35
  14.4 8.6 %all-to-all-start = ((f32[16,2048,96]{1,2,0:T(8,128)}), f32[16,2048,96]{1,2,0:T(8,128)}, u32[]{:S(2)}, u32[]{:S(2)}) async-start(f32[16,2048,96]{1,2,0:T(8,128)} %stack.2), calls=%async_computation | async-start | bytes 25165824 | tf_op jit(solution)/shard_map/all_to_all | solution.py:35
  23.0 0.0 reduce-scatter.2.cloned.1.call-start
  23.1 0.0 copy-done
  23.8 0.0 copy-done.1
  23.9 185.4 %all-to-all-done = f32[16,2048,96]{1,2,0:T(8,128)} async-done(((f32[16,2048,96]{1,2,0:T(8,128)}), f32[16,2048,96]{1,2,0:T(8,128)}, u32[]{:S(2)}, u32[]{:S(2)}) %all-to-all-start) | async-done | bytes 12582944 | tf_op jit(solution)/shard_map/all_to_all | solution.py:35
  209.3 11.2 %copy.20 = f32[16,12,8,2048]{3,2,0,1:T(8,128)} copy(f32[16,12,8,2048]{3,2,1,0:T(8,128)} %bitcast.4) | data formatting | bytes 25165824 | tf_op jit(solution)/shard_map/reshape | solution.py:34
  220.5 25.3 %fusion.1 = f32[128,96]{0,1:T(8,128)S(1)} fusion(f32[32768,96]{0,1:T(8,128)} %bitcast.17, s32[128,32768]{1,0:T(8,128)} %param.5, f32[32768]{0:T(1024)S(1)} %log.19, f32[128]{0:T(128)S(1)} %log_subtract_fusion), kind=kOutput, calls=%fused_computation.2 | convolution fusion | flops 4861198336 | bytes 29540864 | tf_op jit(solution)/shard_map/dot_general | solution.py:32
  245.9 13.9 %all_to_all.10 = f32[8,128,96]{1,2,0:T(8,128)S(1)} all-to-all(f32[8,128,96]{1,2,0:T(8,128)S(1)} %broadcast_in_dim.5), channel_id=1, replica_groups=mesh['row_0'=4,'row_1'=4,'col'=8] {'col'}, dimensions={0} | all-to-all | bytes 786432 | tf_op jit(solution)/shard_map/all_to_all | solution.py:13
  259.8 23.0 %fusion = f32[32768,96]{0,1:T(8,128)} fusion(f32[128,96]{0,1:T(8,128)S(1)} %reduce_sum.9, s32[128,32768]{1,0:T(8,128)} %param.5, f32[32768]{0:T(1024)S(1)} %log.19, f32[128]{0:T(128)S(1)} %log_subtract_fusion), kind=kOutput, calls=%fused_computation.1 | convolution fusion | flops 4861198336 | bytes 29540864 | tf_op jit(solution)/shard_map/dot_general | solution.py:48
  282.8 0.0 reduce-scatter.2.cloned.1.call-update
  282.8 0.2 fusion.21
  283.0 13.4 %psum.14 = f32[96,96]{0,1:T(8,128)S(1)} all-reduce(f32[96,96]{0,1:T(8,128)S(1)} %fusion.21), channel_id=1, replica_groups=mesh['row_0'=4,'row_1'=4,'col'=8] {'row_0'}, use_global_device_ids=true, to_apply=%region_2.3 | all-reduce | flops 9216 | bytes 73728 | tf_op jit(solution)/shard_map/psum | solution.py:22
  296.4 13.5 %psum.15 = f32[96,96]{0,1:T(8,128)S(1)} all-reduce(f32[96,96]{0,1:T(8,128)S(1)} %psum.14), channel_id=1, replica_groups=mesh['row_0'=4,'row_1'=4,'col'=8] {'row_1'}, use_global_device_ids=true, to_apply=%region_3.4 | all-reduce | flops 9216 | bytes 73728 | tf_op jit(solution)/shard_map/psum | solution.py:22
  309.9 0.1 copy.18
  310.0 8.8 %cholesky.16 = f32[96,96]{1,0:T(8,128)S(1)} custom-call(f32[96,96]{1,0:T(8,128)S(1)} %fusion.14), custom_call_target="Cholesky" | custom-call | tf_op jit(solution)/shard_map/jit(cholesky)/cholesky | solution.py:45
  318.8 0.6 compare_reduce_fusion
  319.5 1.3 select_bitcast_fusion
  320.8 7.4 %custom-call.7 = f32[1,96,96]{1,2,0:T(8,128)S(1)} custom-call(f32[1,96,96]{2,1,0:T(8,128)S(1)} %get-tuple-element.2), custom_call_target="InvertDiagBlocksLowerTriangular" | custom-call | tf_op jit(solution)/shard_map/jit(_solve_triangular)/triangular_solve | solution.py:59
  328.1 47.4 %reduce-scatter.2.cloned.1.call-done = f32[2048,96]{0,1:T(8,128)} async-done(((f32[32768,96]{0,1:T(8,128)}), f32[2048,96]{0,1:T(8,128)}) %reduce-scatter.2.cloned.1.call-update) | async-done | bytes 786448 | tf_op jit(solution)/shard_map/reduce_scatter | solution.py:47
  375.6 2.8 fusion.12
  (6 shorter events, 0.1 us)
Async XLA Ops:
  7.2 15.9 %copy-start = (f32[32768]{0:T(1024)S(1)}, f32[32768]{0:T(1024)}, u32[]{:S(2)}) copy-start(f32[32768]{0:T(1024)} %param.7) | copy-start | bytes 393220
  7.2 16.7 %copy-start.1 = (f32[128]{0:T(128)S(1)}, f32[128]{0:T(128)}, u32[]{:S(2)}) copy-start(f32[128]{0:T(128)} %param.6) | copy-start | bytes 1540
  14.4 194.9 %all-to-all-start = ((f32[16,2048,96]{1,2,0:T(8,128)}), f32[16,2048,96]{1,2,0:T(8,128)}, u32[]{:S(2)}, u32[]{:S(2)}) async-start(f32[16,2048,96]{1,2,0:T(8,128)} %stack.2), calls=%async_computation | async-start | bytes 25165824 | tf_op jit(solution)/shard_map/all_to_all | solution.py:35
  23.0 352.5 %reduce-scatter.2.cloned.1.call-start = ((), (), s32[]{:S(2)}) async-start(), calls=%async_computation.3 | async-start | bytes 13369344 | tf_op jit(solution)/shard_map/reduce_scatter | solution.py:47
Sparse Core Ops, SparseCore 0:
  282.9 92.6 reduce-scatter.1
